TPU v7x, 512 devices: a whole 4x4x16 slice. The times are simulated.
512 devices in a mesh: expert: 128 (over x, z_lo, y), dp: 4 (over z_hi, core).
Axes of the slice: x: 4, y: 4, z: 16 (z_hi: 2, z_lo: 8; z = z_hi * 8 + z_lo), core: 2. Of those that a mesh axis runs over, the one named last changes fastest.
Arguments:
- tokens: bfloat16 [8192, 2048], P(('expert', 'dp')), may hold values from -6 to 6
- cotangent: bfloat16 [8192, 2048], P(('expert', 'dp')), may hold values from -6 to 6
- route_ids: int32 [8192, 8], P(('expert', 'dp')), may hold values from 0 to 127, all different within a row; in each aligned block of 16 rows (0 to 15, 16 to 31, ...) at most 2 rows name the same one
- route_gates: bfloat16 [8192, 8], P(('expert', 'dp')), may hold values from 0.019897461 to 0.5
- gate_up: bfloat16 [128, 2048, 1536], P('expert', 'dp'), may hold values from -0.125 to 0.125
- down: bfloat16 [128, 2048, 768], P('expert', 'dp'), may hold values from -6 to 6
- moment1: bfloat16 [128, 2048, 768], P('expert', 'dp'), may hold values from -4 to 4
- moment2: bfloat16 [128, 2048, 768], P('expert', 'dp'), may hold values from 0.049804688 to 0.5
- placement: int32 [128], replicated, may hold values from 0 to 127, each once
Outputs:
- rollout_down: bfloat16 [128, 2048, 768], P('expert', None, 'dp')
Inputs may be any that keep to these rules, and one draw needn't show every extreme that they name: `route_ids`: each row names 8 different experts; within the rows of one device no expert is named more than 2 times, a bound that some block reaches. `placement`: each expert exactly once.
All inputs are finite; a program needn't handle non-finite values.
Results may differ from a plain program's by a relative error of at most 0.003.
Values may be sent and summed in bfloat16 or wider, within the bound.
A program may use at most 64 MiB of HBM per device.

v0:
```python
import jax
import jax.numpy as jnp
from jax import lax
from jax.sharding import Mesh, PartitionSpec as P

OPT_STEP = 2
BETA_ONE = 0.9
BETA_TWO = 0.95
ADAM_EPS = 1e-08
LEARN_RATE = 0.25
DP = ("zh", "core")
PLANE = ("x", "y")
EXPERT = ("x", "zl", "y")
CAP = 2
META = 128
contract_rows = (((0,), (0,)), ((), ()))


def pickers(meta, blocks, block_rows, top):
    plane = lax.axis_size(PLANE)
    wide = meta.shape[0]
    ids = meta[:, :top].astype(jnp.int32)
    gates = meta[:, top : 2 * top].astype(jnp.float32)
    place = jnp.arange(plane, dtype=jnp.int32)
    y_size = lax.axis_size("y")
    wanted = (
        place // y_size * lax.axis_size("zl") + lax.axis_index("zl")
    ) * y_size + place % y_size
    match = (ids[:, :, None] == wanted).astype(jnp.float32)
    hits = jnp.sum(match, axis=1)
    worth = jnp.sum(match * gates[:, :, None], axis=1)
    token = jnp.arange(wide, dtype=jnp.int32)
    own_block = token // block_rows
    before = (
        (own_block[:, None] == own_block[None, :]) & (token[None, :] < token[:, None])
    ).astype(jnp.bfloat16)
    earlier = jnp.dot(before, hits.astype(jnp.bfloat16), preferred_element_type=jnp.float32)
    row = jnp.arange(plane * blocks * CAP, dtype=jnp.int32)
    row_place = row // (blocks * CAP)
    spread = (row_place[:, None] == place[None, :]).astype(jnp.bfloat16)
    take = lambda v: lax.dot_general(
        spread, v.astype(jnp.bfloat16), (((1,), (1,)), ((), ())), preferred_element_type=jnp.float32
    )
    here = (row // CAP % blocks)[:, None] == own_block[None, :]
    slot = jnp.where(hits > 0, earlier, -1.0)
    chosen = here & (take(slot) == (row % CAP)[:, None].astype(jnp.float32))
    one_hot = chosen.astype(jnp.bfloat16)
    return (one_hot, jnp.where(chosen, take(worth), 0.0).astype(jnp.bfloat16))


def shards(tokens, cotangent, route_ids, route_gates, gate_up, down, moment1, moment2, placement):
    tok_rows, width = tokens.shape
    top = route_ids.shape[1]
    hidden_units = down.shape[2]
    groups = lax.axis_size(DP)
    line = lax.axis_size("zl")
    plane = lax.axis_size(PLANE)
    experts = lax.axis_size(EXPERT)
    share = width // groups
    bf16 = jnp.bfloat16
    meta = jnp.concatenate(
        [route_ids.astype(bf16), route_gates, jnp.zeros((tok_rows, META - 2 * top), bf16)], axis=1
    )
    tok_pack = lax.all_gather(jnp.concatenate([tokens, meta], axis=1), "zl", axis=0, tiled=True)
    cot_parts = cotangent.reshape(tok_rows, groups, share).transpose(1, 0, 2)
    cot_parts = jnp.concatenate(
        [cot_parts, jnp.broadcast_to(meta[None], (groups, tok_rows, META))], axis=2
    )
    cot_parts = lax.all_to_all(cot_parts, DP, split_axis=0, concat_axis=0, tiled=True)
    cot_pack = lax.all_gather(
        cot_parts.reshape(groups * tok_rows, share + META), "zl", axis=0, tiled=True
    )
    weights = lax.all_gather(gate_up[0], DP, axis=0, tiled=True)
    tok_pick, _ = pickers(tok_pack[:, width:], line, tok_rows, top)
    rows = jnp.dot(tok_pick, tok_pack[:, :width], preferred_element_type=jnp.float32).astype(bf16)
    rows = lax.all_to_all(
        rows.reshape(plane, line * CAP, width), PLANE, split_axis=0, concat_axis=0, tiled=True
    ).reshape(plane * line * CAP, width)
    _, cot_pick = pickers(cot_pack[:, share:], line * groups, tok_rows, top)
    scaled = jnp.dot(cot_pick, cot_pack[:, :share], preferred_element_type=jnp.float32).astype(bf16)
    scaled = lax.all_to_all(
        scaled.reshape(plane, line * groups * CAP, share),
        PLANE,
        split_axis=0,
        concat_axis=0,
        tiled=True,
    )
    scaled = scaled.reshape(plane * line, groups, CAP, share).transpose(1, 0, 2, 3)
    scaled = scaled.reshape(groups * plane * line * CAP, share)
    pre = jnp.dot(rows, weights, preferred_element_type=jnp.float32)
    hidden = (jax.nn.silu(pre[:, :hidden_units]) * pre[:, hidden_units:]).astype(bf16)
    hidden = lax.all_gather(hidden, DP, axis=0, tiled=True)
    grad = lax.dot_general(scaled, hidden, contract_rows, preferred_element_type=jnp.float32)
    correct_one = 1.0 - BETA_ONE**OPT_STEP
    correct_two = 1.0 - BETA_TWO**OPT_STEP
    first = BETA_ONE * moment1[0].astype(jnp.float32) + (1.0 - BETA_ONE) * grad
    second = BETA_TWO * moment2[0].astype(jnp.float32) + (1.0 - BETA_TWO) * grad * grad
    direction = first / correct_one / (jnp.sqrt(second / correct_two) + ADAM_EPS)
    updated = (down[0].astype(jnp.float32) - LEARN_RATE * direction).astype(bf16)
    block_cols = hidden_units // groups
    piece_rows = share // experts
    pieces = updated.reshape(experts, piece_rows, groups, block_cols).transpose(0, 2, 1, 3)
    pieces = pieces.reshape(experts * groups, piece_rows * block_cols)
    spread = lax.all_to_all(pieces, EXPERT + DP, split_axis=0, concat_axis=0, tiled=True)
    spread = spread.reshape(experts, groups * piece_rows * block_cols)
    picked = jnp.take(spread, placement, axis=0)
    landed = lax.all_to_all(picked, EXPERT, split_axis=0, concat_axis=0, tiled=True)
    landed = landed.reshape(experts, groups, piece_rows, block_cols).transpose(1, 0, 2, 3)
    return landed.reshape(1, width, block_cols)


def solution(mesh):
    grid = Mesh(mesh.devices.reshape(4, 8, 4, 2, 2), EXPERT + DP)
    every = P(EXPERT + DP, None)
    owned = P(EXPERT, DP, None)
    placed = (every, every, every, every, owned, owned, owned, owned, P())
    return jax.shard_map(
        shards, mesh=grid, in_specs=placed, out_specs=P(EXPERT, None, DP), check_vma=False
    )
```

profile of v0, /device:TPU:1, one launch (start us, length us, event | category | flops | bytes accessed | tf_op | source)
XLA Modules:
  0.0 447.6 jit_solution(951209966834745455)
XLA Ops:
  6.5 0.0 copy-start.3
  6.5 0.0 all-gather.6.cloned.1.call-start
  6.5 0.7 all-gather.6.cloned.1.call-update
  7.3 0.0 copy-done.3
  7.3 0.1 copy.84
  7.4 0.0 copy-done.2
  7.4 0.1 copy.83
  7.4 0.0 copy-done
  7.4 0.1 concatenate.12
  7.5 63.2 %all_gather.13 = bf16[128,2176]{1,0:T(8,128)(2,1)S(1)} all-gather(bf16[16,2176]{1,0:T(8,128)(2,1)S(1)} %concatenate.12), channel_id=1, replica_groups=mesh['x'=4,'zl'=8,'y'=4,'zh'=2,'core'=2] {'zl'}, dimensions={0}, use_global_device_ids=true | all-gather | bytes 626688 | tf_op jit(solution)/shard_map/all_gather | solution.py:64
  70.8 0.1 copy.99
  70.9 0.1 convert_reduce_fusion
  71.0 0.2 fusion.14
  71.2 1.6 convolution_convert_fusion
  72.8 5.8 %all-to-all-start.2 = ((bf16[16,16,2048]{2,1,0:T(8,128)(2,1)}), bf16[16,16,2048]{2,1,0:T(8,128)(2,1)S(1)}, u32[]{:S(2)}, u32[]{:S(2)}) async-start(bf16[16,16,2048]{2,1,0:T(8,128)(2,1)} %bitcast.6), calls=%async_computation.2 | async-start | bytes 2097152 | tf_op jit(solution)/shard_map/all_to_all | solution.py:76
  78.6 0.0 copy-done.1
  78.7 0.1 pad_maximum_fusion.1
  78.8 0.6 copy.85
  79.5 11.3 %all-to-all-done.2 = bf16[16,16,2048]{2,1,0:T(8,128)(2,1)S(1)} async-done(((bf16[16,16,2048]{2,1,0:T(8,128)(2,1)}), bf16[16,16,2048]{2,1,0:T(8,128)(2,1)S(1)}, u32[]{:S(2)}, u32[]{:S(2)}) %all-to-all-start.2) | async-done | bytes 1048608 | tf_op jit(solution)/shard_map/all_to_all | solution.py:76
  90.8 78.6 %all-to-all-start = ((bf16[4,16,640]{2,1,0:T(8,128)(2,1)}), bf16[4,16,640]{2,1,0:T(8,128)(2,1)S(1)}, u32[]{:S(2)}, u32[]{:S(2)}) async-start(bf16[4,16,640]{2,1,0:T(8,128)(2,1)} %copy.85), calls=%async_computation | async-start | bytes 163840 | tf_op jit(solution)/shard_map/all_to_all | solution.py:69
  169.4 0.0 all-gather.4.cloned.1.call-start
  169.4 18.9 %all-gather.6.cloned.1.call-done = bf16[1,2048,1536]{2,1,0:T(8,128)(2,1)} async-done(((bf16[1,512,1536]{2,1,0:T(8,128)(2,1)}), bf16[1,2048,1536]{2,1,0:T(8,128)(2,1)}) %all-gather.6.cloned.1.call-update) | async-done | bytes 6291472 | tf_op jit(solution)/shard_map/all_gather | solution.py:73
  188.3 4.6 %fusion = f32[256,1536]{1,0:T(8,128)S(1)} fusion(bf16[256,2048]{1,0:T(8,128)(2,1)S(1)} %bitcast.38, bf16[1,2048,1536]{2,1,0:T(8,128)(2,1)} %all-gather.6.cloned.1.call-done), kind=kOutput, calls=%fused_computation.1 | convolution fusion | flops 1610612736 | bytes 8912896 | tf_op jit(solution)/shard_map/dot_general | solution.py:90
  192.9 1.0 fusion.24
  193.8 0.0 all-gather.4.cloned.1.call-update
  193.9 0.0 all-to-all-done
  193.9 79.7 %all_gather.12 = bf16[512,640]{1,0:T(8,128)(2,1)S(1)} all-gather(bf16[64,640]{1,0:T(8,128)(2,1)S(1)} %bitcast.40), channel_id=1, replica_groups=mesh['x'=4,'zl'=8,'y'=4,'zh'=2,'core'=2] {'zl'}, dimensions={0}, use_global_device_ids=true | all-gather | bytes 737280 | tf_op jit(solution)/shard_map/all_gather | solution.py:70
  273.6 0.1 fusion.81
  273.7 0.1 copy.97
  273.8 0.1 copy.98
  273.9 0.1 fusion.32
  274.0 0.7 fusion.13
  274.7 2.0 convolution_convert_fusion.1
  276.8 20.4 %all_to_all.31 = bf16[16,64,512]{2,1,0:T(8,128)(2,1)S(1)} all-to-all(bf16[16,64,512]{2,1,0:T(8,128)(2,1)} %bitcast.39), channel_id=1, replica_groups=mesh['x'=4,'zl'=8,'y'=4,'zh'=2,'core'=2] {'x','y'}, dimensions={0} | all-to-all | bytes 2097152 | tf_op jit(solution)/shard_map/all_to_all | solution.py:81
  297.1 0.4 reshape.253
  297.6 0.7 copy.88
  298.3 0.0 copy-start.4
  298.3 0.4 reshape.254
  298.7 0.0 all-gather.4.cloned.1.call-done
  298.8 0.6 copy-done.4
  299.4 3.9 fusion.10
  303.3 0.9 reshape.257
  304.2 0.4 copy.91
  304.6 1.8 all_to_all.25
  306.4 0.5 broadcast.427
  306.9 5.4 %reduce.1 = bf16[512,768]{1,0:T(8,128)(2,1)S(1)} reduce(bf16[512,1,768]{2,1,0:T(2,128)(2,1)S(1)} %all_to_all.25, bf16[]{:T(256)} %broadcast.427), dimensions={1}, to_apply=%all_to_all.25.reduce_sub_computation | reduce | bytes 1572866 | tf_op jit(solution)/shard_map/all_to_all | solution.py:104
  312.3 0.0 copy-start.5
  312.4 1.1 reshape.273
  313.4 18.7 %all-to-all-start.3 = ((bf16[512,2,384]{2,1,0:T(2,128)(2,1)}), bf16[512,2,384]{2,1,0:T(2,128)(2,1)S(1)}, u32[]{:S(2)}, u32[]{:S(2)}) async-start(bf16[512,2,384]{2,1,0:T(2,128)(2,1)} %reshape.273), calls=%async_computation.3 | async-start | bytes 1572864 | tf_op jit(solution)/shard_map/all_to_all | solution.py:104
  332.2 0.0 copy-done.5
  332.2 46.2 %all-to-all-done.3 = bf16[512,2,384]{2,1,0:T(2,128)(2,1)S(1)} async-done(((bf16[512,2,384]{2,1,0:T(2,128)(2,1)}), bf16[512,2,384]{2,1,0:T(2,128)(2,1)S(1)}, u32[]{:S(2)}, u32[]{:S(2)}) %all-to-all-start.3) | async-done | bytes 786464 | tf_op jit(solution)/shard_map/all_to_all | solution.py:104
  378.4 0.6 reshape.274
  379.1 5.0 %reduce = bf16[512,768]{1,0:T(8,128)(2,1)S(1)} reduce(bf16[512,1,768]{2,1,0:T(2,128)(2,1)S(1)} %reshape.274, bf16[]{:T(256)} %constant.215), dimensions={1}, to_apply=%all_to_all.23.reduce_sub_computation | reduce | bytes 1572866 | tf_op jit(solution)/shard_map/all_to_all | solution.py:104
  384.1 0.5 reshape.258
  384.5 1.0 gather_fusion
  385.6 0.1 bitcast_select_fusion
  385.7 1.2 reduce.2
  386.9 0.6 reshape.275
  387.5 48.3 %all_to_all.32 = bf16[128,2,1536]{2,1,0:T(2,128)(2,1)S(1)} all-to-all(bf16[128,2,1536]{2,1,0:T(2,128)(2,1)S(1)} %reshape.275), channel_id=1, replica_groups=mesh['x'=4,'zl'=8,'y'=4,'zh'=2,'core'=2] {'x','zl','y'}, dimensions={0} | all-to-all | bytes 1572864 | tf_op jit(solution)/shard_map/all_to_all | solution.py:107
  435.7 0.6 reshape.276
  436.4 1.8 copy.94
  438.1 0.7 copy.95
  438.9 0.7 reshape.260
  439.5 1.2 copy.96
  (22 shorter events, 0.2 us)
Async XLA Ops:
  6.5 0.7 copy-start.3
  6.5 0.8 copy-start.2
  6.5 0.9 copy-start
  6.5 181.8 %all-gather.6.cloned.1.call-start = ((), (), s32[]{:S(2)}) async-start(), calls=%async_computation.6 | async-start | bytes 7864320 | tf_op jit(solution)/shard_map/all_gather | solution.py:73
  71.2 7.5 %copy-start.1 = (bf16[16,2048]{1,0:T(8,128)(2,1)S(1)}, bf16[16,2048]{1,0:T(8,128)(2,1)}, u32[]{:S(2)}) copy-start(bf16[16,2048]{1,0:T(8,128)(2,1)} %param.10) | copy-start | bytes 196612
  72.8 18.0 %all-to-all-start.2 = ((bf16[16,16,2048]{2,1,0:T(8,128)(2,1)}), bf16[16,16,2048]{2,1,0:T(8,128)(2,1)S(1)}, u32[]{:S(2)}, u32[]{:S(2)}) async-start(bf16[16,16,2048]{2,1,0:T(8,128)(2,1)} %bitcast.6), calls=%async_computation.2 | async-start | bytes 2097152 | tf_op jit(solution)/shard_map/all_to_all | solution.py:76
  90.8 103.1 %all-to-all-start = ((bf16[4,16,640]{2,1,0:T(8,128)(2,1)}), bf16[4,16,640]{2,1,0:T(8,128)(2,1)S(1)}, u32[]{:S(2)}, u32[]{:S(2)}) async-start(bf16[4,16,640]{2,1,0:T(8,128)(2,1)} %copy.85), calls=%async_computation | async-start | bytes 163840 | tf_op jit(solution)/shard_map/all_to_all | solution.py:69
  169.4 129.4 %all-gather.4.cloned.1.call-start = ((), (), s32[]{:S(2)}) async-start(), calls=%async_computation.5 | async-start | bytes 1966080 | tf_op jit(solution)/shard_map/all_gather | solution.py:92
  298.3 1.1 copy-start.4
  312.3 19.8 %copy-start.5 = (s32[128]{0:T(128)S(1)}, s32[128]{0:T(128)}, u32[]{:S(2)}) copy-start(s32[128]{0:T(128)} %param.17) | copy-start | bytes 1540
  313.4 65.0 %all-to-all-start.3 = ((bf16[512,2,384]{2,1,0:T(2,128)(2,1)}), bf16[512,2,384]{2,1,0:T(2,128)(2,1)S(1)}, u32[]{:S(2)}, u32[]{:S(2)}) async-start(bf16[512,2,384]{2,1,0:T(2,128)(2,1)} %reshape.273), calls=%async_computation.3 | async-start | bytes 1572864 | tf_op jit(solution)/shard_map/all_to_all | solution.py:104
Sparse Core Ops, SparseCore 0:
  9.4 178.8 all-gather.5
  194.0 86.3 all-gather.3
where the time goes:
time: 448 us
  blocking collectives  212 us (47%)
  starting transfers between devices  103 us (23%)
  waiting for transfers between devices  77.2 us (17%)
  local copies, waits for them, and re-layouts  15.9 us (4%)
  between operations  13.7 us (3%)
  other arithmetic  13.1 us (3%)
  matrix products  13 us (3%)
    all_gather x1, blocking collectives, shards(): lax.all_gather(cot_parts.reshape(groups * tok_rows, share + META), 'zl',...  79.7 us
    all_to_all x1, starting transfers between devices, shards(): lax.all_to_all(cot_parts, DP, split_axis=0, concat_axis=0, tiled=True)  78.6 us
    all_gather x1, blocking collectives, shards(): lax.all_gather(jnp.concatenate([tokens, meta], axis=1), 'zl', axis=0, til...  63.2 us
    all_to_all x1, blocking collectives, shards(): lax.all_to_all(picked, EXPERT, split_axis=0, concat_axis=0, tiled=True)  48.3 us
    all_to_all x1, waiting for transfers between devices, shards(): lax.all_to_all(pieces, EXPERT + DP, split_axis=0, concat_axis=0, tiled=True)  46.2 us
    all_to_all x1, blocking collectives, shards(): lax.all_to_all(scaled.reshape(plane, line * groups * CAP, share), PLANE,...  20.4 us
    all_gather x1, waiting for transfers between devices, shards(): weights = lax.all_gather(gate_up[0], DP, axis=0, tiled=True)  18.9 us
    all_to_all x1, starting transfers between devices, shards(): lax.all_to_all(pieces, EXPERT + DP, split_axis=0, concat_axis=0, tiled=True)  18.7 us
  transfers between devices with their start and end apart: 5, of which 3 were waited for; matrix products, arithmetic and copies ran while one was open for 3% of the time, Pallas kernels for 0%

commit v1 on v0

--- a/solution.py
+++ b/solution.py
@@ -67,8 +67,14 @@
         [cot_parts, jnp.broadcast_to(meta[None], (groups, tok_rows, META))], axis=2
     )
     cot_parts = lax.all_to_all(cot_parts, DP, split_axis=0, concat_axis=0, tiled=True)
-    cot_pack = lax.all_gather(
-        cot_parts.reshape(groups * tok_rows, share + META), "zl", axis=0, tiled=True
+    cot_pack = jnp.concatenate(
+        lax.all_to_all(
+            jnp.stack([cot_parts.reshape(groups * tok_rows, share + META)] * lax.axis_size("zl")),
+            "zl",
+            0,
+            0,
+        ),
+        axis=0,
     )
     weights = lax.all_gather(gate_up[0], DP, axis=0, tiled=True)
     tok_pick, _ = pickers(tok_pack[:, width:], line, tok_rows, top)

time: 448 us -> 412 us (0.920)
  blocking collectives: 212 us -> 156 us
  waiting for transfers between devices: 77.2 us -> 116 us
  starting transfers between devices: 103 us -> 83.9 us
    all_gather x1 -> x0, blocking collectives: 79.7 us -> none  [shards(): lax.all_gather(cot_parts.reshape(groups * tok_rows, share + META), 'zl',...]
    all_to_all x1, starting transfers between devices: 78.6 us -> 16.6 us  [shards(): lax.all_to_all(cot_parts, DP, split_axis=0, concat_axis=0, tiled=True)]
    all_to_all x1, starting transfers between devices: 5.83 us -> 56.8 us  [shards(): lax.all_to_all(jnp.stack([cot_parts.reshape(groups * tok_rows, share + ME...]
    all_gather x1, waiting for transfers between devices: 0.02 us -> 48.6 us  [shards(): hidden = lax.all_gather(hidden, DP, axis=0, tiled=True)]
    all_to_all x0 -> x1, blocking collectives: none -> 22.8 us  [shards(): lax.all_to_all(rows.reshape(plane, line * CAP, width), PLANE, split_axis=...]
    all_to_all x1, waiting for transfers between devices: 11.3 us -> 2.35 us  [shards(): lax.all_to_all(jnp.stack([cot_parts.reshape(groups * tok_rows, share + ME...]
    all_to_all x1, starting transfers between devices: 18.7 us -> 10.5 us  [shards(): lax.all_to_all(pieces, EXPERT + DP, split_axis=0, concat_axis=0, tiled=True)]
  transfers between devices with their start and end apart: 5 -> 5, of which waited for: 3 -> 4; matrix products, arithmetic and copies ran while one was open for 3% -> 3% of each run, Pallas kernels for 0% -> 0%
where the time goes in v1:
time: 412 us; the launch traced here: 411 us
  blocking collectives  156 us (38%)
  waiting for transfers between devices  116 us (28%)
  starting transfers between devices  83.9 us (20%)
  local copies, waits for them, and re-layouts  16.1 us (4%)
  between operations  13.7 us (3%)
  other arithmetic  13.1 us (3%)
  matrix products  12 us (3%)
    all_gather x1, blocking collectives, shards(): lax.all_gather(jnp.concatenate([tokens, meta], axis=1), 'zl', axis=0, til...  67 us
    all_to_all x1, starting transfers between devices, shards(): lax.all_to_all(jnp.stack([cot_parts.reshape(groups * tok_rows, share + ME...  56.8 us
    all_gather x1, waiting for transfers between devices, shards(): hidden = lax.all_gather(hidden, DP, axis=0, tiled=True)  48.6 us
    all_to_all x1, blocking collectives, shards(): lax.all_to_all(picked, EXPERT, split_axis=0, concat_axis=0, tiled=True)  48.3 us
    all_to_all x1, waiting for transfers between devices, shards(): lax.all_to_all(pieces, EXPERT + DP, split_axis=0, concat_axis=0, tiled=True)  46.2 us
    all_to_all x1, blocking collectives, shards(): lax.all_to_all(rows.reshape(plane, line * CAP, width), PLANE, split_axis=...  22.8 us
    all_to_all x1, blocking collectives, shards(): lax.all_to_all(scaled.reshape(plane, line * groups * CAP, share), PLANE,...  18.1 us
    all_gather x1, waiting for transfers between devices, shards(): weights = lax.all_gather(gate_up[0], DP, axis=0, tiled=True)  18 us
  transfers between devices with their start and end apart: 5, of which 4 were waited for; matrix products, arithmetic and copies ran while one was open for 3% of the time, Pallas kernels for 0%

profile of v1, /device:TPU:1, one launch (start us, length us, event | category | flops | bytes accessed | tf_op | source)
XLA Modules:
  0.0 411.0 jit_solution(6388951015111669551)
XLA Ops:
  6.5 0.0 all-gather.6.cloned.1.call-start
  6.6 0.7 all-gather.6.cloned.1.call-update
  7.3 0.0 copy-done.3
  7.3 0.1 copy.99
  7.4 0.0 copy-done.2
  7.4 0.1 copy.98
  7.4 0.0 copy-done
  7.5 0.1 pad_maximum_fusion.1
  7.6 0.6 copy.100
  8.3 16.6 %all-to-all-start = ((bf16[4,16,640]{2,1,0:T(8,128)(2,1)}), bf16[4,16,640]{2,1,0:T(8,128)(2,1)S(1)}, u32[]{:S(2)}, u32[]{:S(2)}) async-start(bf16[4,16,640]{2,1,0:T(8,128)(2,1)} %copy.100), calls=%async_computation | async-start | bytes 163840 | tf_op jit(solution)/shard_map/all_to_all | solution.py:69
  24.9 0.0 copy-done.1
  24.9 0.1 concatenate.12
  25.0 67.0 %all_gather.9 = bf16[128,2176]{1,0:T(8,128)(2,1)S(1)} all-gather(bf16[16,2176]{1,0:T(8,128)(2,1)S(1)} %concatenate.12), channel_id=1, replica_groups=mesh['x'=4,'zl'=8,'y'=4,'zh'=2,'core'=2] {'zl'}, dimensions={0}, use_global_device_ids=true | all-gather | bytes 626688 | tf_op jit(solution)/shard_map/all_gather | solution.py:64
  92.0 0.1 copy.114
  92.1 0.1 convert_reduce_fusion
  92.2 0.2 fusion.14
  92.4 0.6 convolution_convert_fusion
  93.0 0.0 all-to-all-done
  93.0 22.8 %all_to_all.36 = bf16[16,16,2048]{2,1,0:T(8,128)(2,1)S(1)} all-to-all(bf16[16,16,2048]{2,1,0:T(8,128)(2,1)S(1)} %bitcast.37), channel_id=1, replica_groups=mesh['x'=4,'zl'=8,'y'=4,'zh'=2,'core'=2] {'x','y'}, dimensions={0} | all-to-all | bytes 2097152 | tf_op jit(solution)/shard_map/all_to_all | solution.py:82
  115.9 0.9 stack.3
  116.7 56.8 %all-to-all-start.1 = ((bf16[8,64,640]{2,1,0:T(8,128)(2,1)}), bf16[8,64,640]{2,1,0:T(8,128)(2,1)S(1)}, u32[]{:S(2)}, u32[]{:S(2)}) async-start(bf16[8,64,640]{2,1,0:T(8,128)(2,1)} %stack.3), calls=%async_computation.1 | async-start | bytes 1310720 | tf_op jit(solution)/shard_map/all_to_all | solution.py:71
  173.6 0.0 all-gather.4.cloned.1.call-start
  173.6 18.0 %all-gather.6.cloned.1.call-done = bf16[1,2048,1536]{2,1,0:T(8,128)(2,1)} async-done(((bf16[1,512,1536]{2,1,0:T(8,128)(2,1)}), bf16[1,2048,1536]{2,1,0:T(8,128)(2,1)}) %all-gather.6.cloned.1.call-update) | async-done | bytes 6291472 | tf_op jit(solution)/shard_map/all_gather | solution.py:79
  191.6 4.6 %fusion = f32[256,1536]{1,0:T(8,128)S(1)} fusion(bf16[256,2048]{1,0:T(8,128)(2,1)S(1)} %bitcast.42, bf16[1,2048,1536]{2,1,0:T(8,128)(2,1)} %all-gather.6.cloned.1.call-done), kind=kOutput, calls=%fused_computation.1 | convolution fusion | flops 1610612736 | bytes 8912896 | tf_op jit(solution)/shard_map/dot_general | solution.py:96
  196.1 1.0 fusion.24
  197.2 0.0 all-gather.4.cloned.1.call-update
  197.2 2.4 all-to-all-done.1
  199.6 0.1 fusion.81
  199.7 0.1 copy.112
  199.8 0.1 copy.113
  199.8 0.1 fusion.32
  200.0 0.7 fusion.13
  200.7 2.0 convolution_convert_fusion.1
  202.7 18.1 %all_to_all.37 = bf16[16,64,512]{2,1,0:T(8,128)(2,1)S(1)} all-to-all(bf16[16,64,512]{2,1,0:T(8,128)(2,1)} %bitcast.43), channel_id=1, replica_groups=mesh['x'=4,'zl'=8,'y'=4,'zh'=2,'core'=2] {'x','y'}, dimensions={0} | all-to-all | bytes 2097152 | tf_op jit(solution)/shard_map/all_to_all | solution.py:87
  220.8 0.4 reshape.255
  221.3 0.7 copy.103
  222.0 0.0 copy-start.4
  222.0 0.4 reshape.256
  222.5 48.6 %all-gather.4.cloned.1.call-done = bf16[1024,768]{1,0:T(8,128)(2,1)} async-done(((bf16[256,768]{1,0:T(8,128)(2,1)}), bf16[1024,768]{1,0:T(8,128)(2,1)}) %all-gather.4.cloned.1.call-update) | async-done | bytes 1572880 | tf_op jit(solution)/shard_map/all_gather | solution.py:98
  271.1 0.0 copy-done.4
  271.1 3.9 fusion.10
  275.0 0.9 reshape.259
  275.9 0.4 copy.106
  276.3 1.8 all_to_all.29
  278.1 0.5 broadcast.428
  278.6 5.4 %reduce.1 = bf16[512,768]{1,0:T(8,128)(2,1)S(1)} reduce(bf16[512,1,768]{2,1,0:T(2,128)(2,1)S(1)} %all_to_all.29, bf16[]{:T(256)} %broadcast.428), dimensions={1}, to_apply=%all_to_all.29.reduce_sub_computation | reduce | bytes 1572866 | tf_op jit(solution)/shard_map/all_to_all | solution.py:110
  284.0 0.0 copy-start.5
  284.0 1.1 reshape.275
  285.1 10.5 %all-to-all-start.4 = ((bf16[512,2,384]{2,1,0:T(2,128)(2,1)}), bf16[512,2,384]{2,1,0:T(2,128)(2,1)S(1)}, u32[]{:S(2)}, u32[]{:S(2)}) async-start(bf16[512,2,384]{2,1,0:T(2,128)(2,1)} %reshape.275), calls=%async_computation.4 | async-start | bytes 1572864 | tf_op jit(solution)/shard_map/all_to_all | solution.py:110
  295.6 0.0 copy-done.5
  295.6 46.2 %all-to-all-done.4 = bf16[512,2,384]{2,1,0:T(2,128)(2,1)S(1)} async-done(((bf16[512,2,384]{2,1,0:T(2,128)(2,1)}), bf16[512,2,384]{2,1,0:T(2,128)(2,1)S(1)}, u32[]{:S(2)}, u32[]{:S(2)}) %all-to-all-start.4) | async-done | bytes 786464 | tf_op jit(solution)/shard_map/all_to_all | solution.py:110
  341.9 0.6 reshape.276
  342.5 5.0 %reduce = bf16[512,768]{1,0:T(8,128)(2,1)S(1)} reduce(bf16[512,1,768]{2,1,0:T(2,128)(2,1)S(1)} %reshape.276, bf16[]{:T(256)} %constant.215), dimensions={1}, to_apply=%all_to_all.27.reduce_sub_computation | reduce | bytes 1572866 | tf_op jit(solution)/shard_map/all_to_all | solution.py:110
  347.5 0.5 reshape.260
  348.0 1.0 gather_fusion
  349.0 0.1 bitcast_select_fusion
  349.1 1.2 reduce.2
  350.3 0.6 reshape.277
  350.9 48.3 %all_to_all.38 = bf16[128,2,1536]{2,1,0:T(2,128)(2,1)S(1)} all-to-all(bf16[128,2,1536]{2,1,0:T(2,128)(2,1)S(1)} %reshape.277), channel_id=1, replica_groups=mesh['x'=4,'zl'=8,'y'=4,'zh'=2,'core'=2] {'x','zl','y'}, dimensions={0} | all-to-all | bytes 1572864 | tf_op jit(solution)/shard_map/all_to_all | solution.py:113
  399.1 0.6 reshape.278
  399.8 1.8 copy.109
  401.6 0.7 copy.110
  402.3 0.7 reshape.262
  403.0 1.2 copy.111
  (23 shorter events, 0.2 us)
Async XLA Ops:
  6.5 0.7 copy-start.3
  6.5 0.8 copy-start.2
  6.5 0.9 copy-start
  6.5 18.3 %copy-start.1 = (bf16[16,2048]{1,0:T(8,128)(2,1)S(1)}, bf16[16,2048]{1,0:T(8,128)(2,1)}, u32[]{:S(2)}) copy-start(bf16[16,2048]{1,0:T(8,128)(2,1)} %param.9) | copy-start | bytes 196612
  6.5 185.0 %all-gather.6.cloned.1.call-start = ((), (), s32[]{:S(2)}) async-start(), calls=%async_computation.7 | async-start | bytes 7864320 | tf_op jit(solution)/shard_map/all_gather | solution.py:79
  8.3 84.7 %all-to-all-start = ((bf16[4,16,640]{2,1,0:T(8,128)(2,1)}), bf16[4,16,640]{2,1,0:T(8,128)(2,1)S(1)}, u32[]{:S(2)}, u32[]{:S(2)}) async-start(bf16[4,16,640]{2,1,0:T(8,128)(2,1)} %copy.100), calls=%async_computation | async-start | bytes 163840 | tf_op jit(solution)/shard_map/all_to_all | solution.py:69
  116.7 82.8 %all-to-all-start.1 = ((bf16[8,64,640]{2,1,0:T(8,128)(2,1)}), bf16[8,64,640]{2,1,0:T(8,128)(2,1)S(1)}, u32[]{:S(2)}, u32[]{:S(2)}) async-start(bf16[8,64,640]{2,1,0:T(8,128)(2,1)} %stack.3), calls=%async_computation.1 | async-start | bytes 1310720 | tf_op jit(solution)/shard_map/all_to_all | solution.py:71
  173.6 97.5 %all-gather.4.cloned.1.call-start = ((), (), s32[]{:S(2)}) async-start(), calls=%async_computation.6 | async-start | bytes 1966080 | tf_op jit(solution)/shard_map/all_gather | solution.py:98
  222.0 49.1 %copy-start.4 = (bf16[1,512,768]{2,1,0:T(8,128)(2,1)S(1)}, bf16[1,512,768]{2,1,0:T(8,128)(2,1)}, u32[]{:S(2)}) copy-start(bf16[1,512,768]{2,1,0:T(8,128)(2,1)} %param.16) | copy-start | bytes 2359300
  284.0 11.6 %copy-start.5 = (s32[128]{0:T(128)S(1)}, s32[128]{0:T(128)}, u32[]{:S(2)}) copy-start(s32[128]{0:T(128)} %param.17) | copy-start | bytes 1540
  285.1 56.8 %all-to-all-start.4 = ((bf16[512,2,384]{2,1,0:T(2,128)(2,1)}), bf16[512,2,384]{2,1,0:T(2,128)(2,1)S(1)}, u32[]{:S(2)}, u32[]{:S(2)}) async-start(bf16[512,2,384]{2,1,0:T(2,128)(2,1)} %reshape.275), calls=%async_computation.4 | async-start | bytes 1572864 | tf_op jit(solution)/shard_map/all_to_all | solution.py:110
Sparse Core Ops, SparseCore 0:
  9.5 182.0 all-gather.5
  197.3 73.7 all-gather.3
